TPU v7x, 512 devices: a whole 4x4x16 slice. The times are simulated.
512 devices in a mesh: rep: 4 (over y), shard: 32 (over z, core), tp: 4 (over x).
Axes of the slice: x: 4, y: 4, z: 16, core: 2. Of those that a mesh axis runs over, the one named last changes fastest.
Arguments:
- qkv_grad: bfloat16 [4, 1024, 3072], P('rep', 'shard', 'tp'), may hold values from -100 to 100
- qkv_error: float32 [4, 1024, 3072], P('rep', 'shard', 'tp'), may hold values from -4 to 4
- qkv_basis: float32 [3072, 32], P('tp'), may hold values from -6 to 6
- qkv_weight: float32 [32, 4, 8, 3072], P('shard', 'rep', None, 'tp'), may hold values from -0.75 to 0.75
- qkv_moment: float32 [32, 4, 8, 3072], P('shard', 'rep', None, 'tp'), may hold values from -0.75 to 0.75
- gu_grad: bfloat16 [4, 1024, 8192], P('rep', 'shard', 'tp'), may hold values from -100 to 100
- gu_error: float32 [4, 1024, 8192], P('rep', 'shard', 'tp'), may hold values from -4 to 4
- gu_basis: float32 [8192, 32], P('tp'), may hold values from -6 to 6
- gu_weight: float32 [32, 4, 8, 8192], P('shard', 'rep', None, 'tp'), may hold values from -0.75 to 0.75
- gu_moment: float32 [32, 4, 8, 8192], P('shard', 'rep', None, 'tp'), may hold values from -0.75 to 0.75
- down_grad: bfloat16 [4, 4096, 1024], P('rep', 'shard', 'tp'), may hold values from -100 to 100
- down_error: float32 [4, 4096, 1024], P('rep', 'shard', 'tp'), may hold values from -4 to 4
- down_basis: float32 [1024, 32], P('tp'), may hold values from -6 to 6
- down_weight: float32 [32, 4, 32, 1024], P('shard', 'rep', None, 'tp'), may hold values from -0.75 to 0.75
- down_moment: float32 [32, 4, 32, 1024], P('shard', 'rep', None, 'tp'), may hold values from -0.75 to 0.75
- vec_grad: bfloat16 [4, 11264], P('rep', ('shard', 'tp')), may hold values from -6 to 6
- vec_weight: float32 [11264], P(('shard', 'tp')), may hold values from 0.5 to 1.5
- vec_moment: float32 [11264], P(('shard', 'tp')), may hold values from -6 to 6
- emb_ids: int32 [4, 4096], P('rep', 'shard'), may hold values from 0 to 31999
- emb_grad: bfloat16 [4, 4096, 1024], P('rep', 'shard', 'tp'), may hold values from -6 to 6
- emb_weight: float32 [32, 4, 250, 1024], P('shard', 'rep', None, 'tp'), may hold values from -0.75 to 0.75
- emb_moment: float32 [32, 4, 250, 1024], P('shard', 'rep', None, 'tp'), may hold values from -6 to 6
Outputs:
- qkv_new: float32 [1024, 3072], P('shard', 'tp')
- qkv_error_new: float32 [4, 1024, 3072], P('rep', 'shard', 'tp')
- qkv_moment_new: float32 [32, 4, 8, 3072], P('shard', 'rep', None, 'tp')
- gu_new: float32 [1024, 8192], P('shard', 'tp')
- gu_error_new: float32 [4, 1024, 8192], P('rep', 'shard', 'tp')
- gu_moment_new: float32 [32, 4, 8, 8192], P('shard', 'rep', None, 'tp')
- down_new: float32 [4096, 1024], P('shard', 'tp')
- down_error_new: float32 [4, 4096, 1024], P('rep', 'shard', 'tp')
- down_moment_new: float32 [32, 4, 32, 1024], P('shard', 'rep', None, 'tp')
- vec_new: float32 [11264], P(('shard', 'tp'))
- vec_moment_new: float32 [11264], P(('shard', 'tp'))
- emb_new: float32 [32000, 1024], P('shard', 'tp')
- emb_moment_new: float32 [32, 4, 250, 1024], P('shard', 'rep', None, 'tp')
All inputs are finite; a program needn't handle non-finite values.
Results may differ from a plain program's by a relative error of at most 0.0004.
Values may be sent and summed in bfloat16 or wider, within the bound.
A program may use at most 64 MiB of HBM per device.

v0:
```python
import jax
import jax.numpy as jnp
from jax import lax
from jax.sharding import PartitionSpec as P

ROUNDS = 2
momentum_decay = 0.9
step_size = 0.05


def solve_right(lower_factor, values):
    return jax.scipy.linalg.solve_triangular(lower_factor, values.T, lower=True).T


def dot_high(left_side, right_side):
    return jnp.dot(left_side, right_side, precision=lax.Precision.HIGHEST)


def add_rows(running, row_ids, row_values, row_start, block_rows):

    def one_block(partial_sum, block_ids, block_values):
        local_ids = block_ids - row_start
        one_hot = (
            local_ids[None, :]
            == lax.broadcasted_iota(jnp.int32, (block_rows, block_ids.shape[0]), 0)
        ).astype(jnp.bfloat16)
        return partial_sum + jnp.dot(one_hot, block_values, preferred_element_type=jnp.float32)

    count = row_ids.shape[0]
    width = 512
    split_ids = row_ids.reshape(count // width, width)
    split_values = row_values.reshape(count // width, width, row_values.shape[-1])

    def scan_step(partial_sum, inputs):
        return (one_block(partial_sum, inputs[0], inputs[1]), None)

    return lax.scan(scan_step, running, (split_ids, split_values))[0]


def on_device(
    qkv_grad,
    qkv_error,
    qkv_basis,
    qkv_weight,
    qkv_moment,
    gu_grad,
    gu_error,
    gu_basis,
    gu_weight,
    gu_moment,
    down_grad,
    down_error,
    down_basis,
    down_weight,
    down_moment,
    vec_grad,
    vec_weight,
    vec_moment,
    emb_ids,
    emb_grad,
    emb_weight,
    emb_moment,
):
    rep_count = lax.axis_size("rep")
    rep_index = lax.axis_index("rep")
    shard_index = lax.axis_index("shard")
    fulls = [
        qkv_grad[0].astype(jnp.float32) + qkv_error[0],
        gu_grad[0].astype(jnp.float32) + gu_error[0],
        down_grad[0].astype(jnp.float32) + down_error[0],
    ]
    rights = [qkv_basis, gu_basis, down_basis]
    lefts = rights
    for round_index in range(ROUNDS):
        parts = [
            dot_high(full_grad, right_factor) for full_grad, right_factor in zip(fulls, rights)
        ]
        lefts = [lax.psum(left_part, ("rep", "tp")) for left_part in parts]
        grams = [dot_high(left_factor.T, left_factor) for left_factor in lefts]
        summed = lax.psum((grams[0], grams[1], grams[2]), "shard")
        lowers = [jnp.linalg.cholesky(summed[index]) for index in range(3)]
        lefts = [solve_right(lowers[index], lefts[index]) for index in range(3)]
        raw_rights = [
            dot_high(full_grad.T, left_factor) for full_grad, left_factor in zip(fulls, lefts)
        ]
        rights = list(lax.psum((raw_rights[0], raw_rights[1], raw_rights[2]), ("rep", "shard")))
    errors_new = []
    moments_new = []
    flats_new = []
    for index, (weight, moment) in enumerate(
        ((qkv_weight, qkv_moment), (gu_weight, gu_moment), (down_weight, down_moment))
    ):
        approx = dot_high(lefts[index], rights[index].T) / rep_count
        errors_new.append((fulls[index] - approx)[None])
        local_rows = weight.shape[2]
        own_rows = lax.dynamic_slice_in_dim(approx, rep_index * local_rows, local_rows, 0)
        moment_new = momentum_decay * moment[0, 0] + own_rows
        moments_new.append(moment_new[None, None])
        flats_new.append((weight[0, 0] - step_size * moment_new)[None, None])
    vec_mean = lax.psum(vec_grad[0].astype(jnp.float32), "rep") / rep_count
    vec_moment_new = momentum_decay * vec_moment + vec_mean
    vec_new = vec_weight - step_size * vec_moment_new
    block_rows = emb_weight.shape[2]
    row_width = emb_grad.shape[2]
    row_start = (shard_index * rep_count + rep_index) * block_rows
    initial = jnp.zeros((block_rows, row_width), jnp.float32)
    pieces = (
        lax.all_gather(emb_ids, ("rep", "shard"), axis=1, tiled=True),
        lax.all_gather(emb_grad, ("rep", "shard"), axis=1, tiled=True),
    )
    row_ids = pieces[0].reshape(-1)
    row_values = pieces[1].reshape(-1, pieces[1].shape[-1])
    emb_sum = add_rows(initial, row_ids, row_values, row_start, block_rows) / rep_count
    emb_moment_new = momentum_decay * emb_moment[0, 0] + emb_sum
    emb_flat_new = (emb_weight[0, 0] - step_size * emb_moment_new)[None, None]
    gathered = (
        lax.all_gather(flats_new[0], "rep", axis=1, tiled=True),
        lax.all_gather(flats_new[1], "rep", axis=1, tiled=True),
        lax.all_gather(flats_new[2], "rep", axis=1, tiled=True),
        lax.all_gather(emb_flat_new, "rep", axis=1, tiled=True),
    )
    plains = [whole.reshape(whole.shape[1] * whole.shape[2], whole.shape[3]) for whole in gathered]
    return (
        plains[0],
        errors_new[0],
        moments_new[0],
        plains[1],
        errors_new[1],
        moments_new[1],
        plains[2],
        errors_new[2],
        moments_new[2],
        vec_new,
        vec_moment_new,
        plains[3],
        emb_moment_new[None, None],
    )


def solution(mesh):
    return jax.shard_map(
        on_device,
        mesh=mesh,
        in_specs=(
            P("rep", "shard", "tp"),
            P("rep", "shard", "tp"),
            P("tp", None),
            P("shard", "rep", None, "tp"),
            P("shard", "rep", None, "tp"),
            P("rep", "shard", "tp"),
            P("rep", "shard", "tp"),
            P("tp", None),
            P("shard", "rep", None, "tp"),
            P("shard", "rep", None, "tp"),
            P("rep", "shard", "tp"),
            P("rep", "shard", "tp"),
            P("tp", None),
            P("shard", "rep", None, "tp"),
            P("shard", "rep", None, "tp"),
            P("rep", ("shard", "tp")),
            P(("shard", "tp")),
            P(("shard", "tp")),
            P("rep", "shard"),
            P("rep", "shard", "tp"),
            P("shard", "rep", None, "tp"),
            P("shard", "rep", None, "tp"),
        ),
        out_specs=(
            P("shard", "tp"),
            P("rep", "shard", "tp"),
            P("shard", "rep", None, "tp"),
            P("shard", "tp"),
            P("rep", "shard", "tp"),
            P("shard", "rep", None, "tp"),
            P("shard", "tp"),
            P("rep", "shard", "tp"),
            P("shard", "rep", None, "tp"),
            P(("shard", "tp")),
            P(("shard", "tp")),
            P("shard", "tp"),
            P("shard", "rep", None, "tp"),
        ),
        check_vma=False,
    )
```

profile of v0, /device:TPU:16, one launch (start us, length us, event | category | flops | bytes accessed | tf_op | source)
XLA Modules:
  0.0 1575.1 jit_solution(1362675693380436460)
XLA Ops:
  11.9 62.7 %all-reduce.5 = (f32[32,32]{1,0:T(8,128)S(1)}, f32[32,32]{1,0:T(8,128)S(1)}, f32[128,32]{0,1:T(8,128)S(1)}) all-reduce(f32[32,32]{1,0:T(8,128)S(1)} %fusion.29, f32[32,32]{1,0:T(8,128)S(1)} %fusion.11, f32[128,32]{0,1:T(8,128)S(1)} %fusion.20), channel_id=1, replica_groups=mesh['rep'=4,'shard'=32,'tp'=4] {'rep','tp'}, use_global_device_ids=true, to_apply=%region_0.0 | all-reduce | flops 6144 | bytes 49152 | tf_op jit(solution)/shard_map/psum | solution.py:78
  75.1 96.4 %all-reduce.3 = (f32[32,32]{0,1:T(8,128)S(1)}, f32[32,32]{0,1:T(8,128)S(1)}, f32[32,32]{0,1:T(8,128)S(1)}) all-reduce(f32[32,32]{0,1:T(8,128)S(1)} %fusion.68, f32[32,32]{0,1:T(8,128)S(1)} %fusion.70, f32[32,32]{0,1:T(8,128)S(1)} %fusion.72), channel_id=1, replica_groups=mesh['rep'=4,'shard'=32,'tp'=4] {'shard'}, use_global_device_ids=true, to_apply=%region_1.0 | all-reduce | flops 3072 | bytes 24576 | tf_op jit(solution)/shard_map/psum | solution.py:80
  171.7 2.9 cholesky.126
  176.0 2.4 custom-call.15
  178.7 2.1 fusion.9
  180.8 2.9 cholesky.104
  185.1 2.4 custom-call.13
  187.7 1.8 fusion.27
  189.6 2.9 cholesky.148
  193.8 2.4 custom-call.17
  197.6 418.9 %psum.147 = f32[256,32]{0,1:T(8,128)S(1)} all-reduce(f32[256,32]{0,1:T(8,128)S(1)} %fusion.18), channel_id=1, replica_groups=mesh['rep'=4,'shard'=32,'tp'=4] {'rep','shard'}, use_global_device_ids=true, to_apply=%region_16.0 | all-reduce | flops 8192 | bytes 65536 | tf_op jit(solution)/shard_map/psum | solution.py:86
  618.9 1.4 fusion.7
  620.3 141.7 %all-reduce.4 = (f32[32,32]{1,0:T(8,128)S(1)}, f32[32,32]{1,0:T(8,128)S(1)}, f32[128,32]{0,1:T(8,128)S(1)}) all-reduce(f32[32,32]{1,0:T(8,128)S(1)} %fusion.25, f32[32,32]{1,0:T(8,128)S(1)} %fusion.7, f32[128,32]{0,1:T(8,128)S(1)} %fusion.16), channel_id=1, replica_groups=mesh['rep'=4,'shard'=32,'tp'=4] {'rep','tp'}, use_global_device_ids=true, to_apply=%region_5.8 | all-reduce | flops 6144 | bytes 49152 | tf_op jit(solution)/shard_map/psum | solution.py:78
  762.6 90.1 %all-reduce.2 = (f32[32,32]{0,1:T(8,128)S(1)}, f32[32,32]{0,1:T(8,128)S(1)}, f32[32,32]{0,1:T(8,128)S(1)}) all-reduce(f32[32,32]{0,1:T(8,128)S(1)} %fusion.69, f32[32,32]{0,1:T(8,128)S(1)} %fusion.71, f32[32,32]{0,1:T(8,128)S(1)} %fusion.73), channel_id=1, replica_groups=mesh['rep'=4,'shard'=32,'tp'=4] {'shard'}, use_global_device_ids=true, to_apply=%region_6.9 | all-reduce | flops 3072 | bytes 24576 | tf_op jit(solution)/shard_map/psum | solution.py:80
  852.7 2.9 cholesky.137
  857.0 2.4 custom-call.16
  859.6 2.1 fusion.5
  861.8 2.9 cholesky.115
  866.0 2.4 custom-call.14
  868.7 1.8 fusion.23
  871.3 82.0 %all_gather.21 = s32[1,16384]{1,0:T(1,128)S(1)} all-gather(s32[1,128]{1,0:T(1,128)} %param.47), channel_id=1, replica_groups=mesh['rep'=4,'shard'=32,'tp'=4] {'rep','shard'}, dimensions={1}, use_global_device_ids=true | all-gather | bytes 66048 | tf_op jit(solution)/shard_map/all_gather | solution.py:108
  955.2 9.1 psum.151
  965.7 2.9 cholesky.159
  969.9 2.4 custom-call.18
  973.7 415.1 %psum.150 = f32[256,32]{0,1:T(8,128)S(1)} all-reduce(f32[256,32]{0,1:T(8,128)S(1)} %fusion.14), channel_id=1, replica_groups=mesh['rep'=4,'shard'=32,'tp'=4] {'rep','shard'}, use_global_device_ids=true, to_apply=%region_19.23 | all-reduce | flops 8192 | bytes 65536 | tf_op jit(solution)/shard_map/psum | solution.py:86
  1389.1 1.4 fusion.66
  1390.5 88.8 %all-gather.2 = f32[128,256]{1,0:T(8,128)S(1)} all-gather(f32[32,256]{1,0:T(8,128)S(1)} %get-tuple-element.108), channel_id=4, replica_groups=mesh['rep'=4,'shard'=32,'tp'=4] {'rep'}, dimensions={0}, use_global_device_ids=true | all-gather | bytes 163840 | tf_op jit(solution)/shard_map/all_gather | solution.py:119
  1479.3 1.6 fusion.22
  1483.0 12.2 all-gather.1
  1497.0 11.9 all-gather
  1510.4 40.2 %while.11 = (s32[]{:T(128)}, f32[250,256]{1,0:T(8,128)S(1)}, s32[32,512]{1,0:T(8,128)S(1)}, s32[]{:T(128)}, bf16[32,512,256]{2,1,0:T(8,128)(2,1)}, /*index=5*/s32[]{:T(128)}, s32[]{:T(128)}) while((s32[]{:T(128)}, f32[250,256]{1,0:T(8,128)S(1)}, s32[32,512]{1,0:T(8,128)S(1)}, s32[]{:T(128)}, bf16[32,512,256]{2,1,0:T(8,128)(2,1)}, ...), condition=%wide.region_22.26_spmd.clone, body=%wide.region_21.25_spmd.clone.sunk | while | flops 65792512 | bytes 780895 | solution.py:37
  1550.7 13.8 all-gather.4
  (162 shorter events, 72.8 us)
Async XLA Ops:
  7.2 1.0 copy-start
  7.2 1502.4 %copy-start.2 = (bf16[1,32,2048]{2,1,0:T(8,128)(2,1)S(1)}, bf16[1,32,2048]{2,1,0:T(8,128)(2,1)}, u32[]{:S(2)}) copy-start(bf16[1,32,2048]{2,1,0:T(8,128)(2,1)} %param.34) | copy-start | bytes 393220
  7.2 1502.4 %copy-start.1 = (f32[1,32,2048]{2,1,0:T(8,128)S(1)}, f32[1,32,2048]{2,1,0:T(8,128)}, u32[]{:S(2)}) copy-start(f32[1,32,2048]{2,1,0:T(8,128)} %param.35) | copy-start | bytes 786436
  7.2 1501.7 %copy-start.4 = (bf16[1,32,768]{2,1,0:T(8,128)(2,1)S(1)}, bf16[1,32,768]{2,1,0:T(8,128)(2,1)}, u32[]{:S(2)}) copy-start(bf16[1,32,768]{2,1,0:T(8,128)(2,1)} %param.29) | copy-start | bytes 147460
  7.2 1501.7 %copy-start.3 = (f32[1,32,768]{2,1,0:T(8,128)S(1)}, f32[1,32,768]{2,1,0:T(8,128)}, u32[]{:S(2)}) copy-start(f32[1,32,768]{2,1,0:T(8,128)} %param.30) | copy-start | bytes 294916
  7.2 1475.0 %copy-start.8 = (f32[1,1,8,2048]{3,2,1,0:T(8,128)S(1)}, f32[1,1,8,2048]{3,2,1,0:T(8,128)}, u32[]{:S(2)}) copy-start(f32[1,1,8,2048]{3,2,1,0:T(8,128)} %param.37) | copy-start | bytes 196612
  7.3 1475.0 %copy-start.7 = (f32[1,1,8,2048]{3,2,1,0:T(8,128)S(1)}, f32[1,1,8,2048]{3,2,1,0:T(8,128)}, u32[]{:S(2)}) copy-start(f32[1,1,8,2048]{3,2,1,0:T(8,128)} %param.38) | copy-start | bytes 196612
  7.3 1489.1 %copy-start.10 = (f32[1,1,8,768]{3,2,1,0:T(8,128)S(1)}, f32[1,1,8,768]{3,2,1,0:T(8,128)}, u32[]{:S(2)}) copy-start(f32[1,1,8,768]{3,2,1,0:T(8,128)} %param.32) | copy-start | bytes 73732
  7.3 1489.1 %copy-start.9 = (f32[1,1,8,768]{3,2,1,0:T(8,128)S(1)}, f32[1,1,8,768]{3,2,1,0:T(8,128)}, u32[]{:S(2)}) copy-start(f32[1,1,8,768]{3,2,1,0:T(8,128)} %param.33) | copy-start | bytes 73732
  7.3 1543.3 %copy-start.6 = (f32[1,1,250,256]{3,1,2,0:T(1,128)S(1)}, f32[1,1,250,256]{3,1,2,0:T(1,128)}, u32[]{:S(2)}) copy-start(f32[1,1,250,256]{3,1,2,0:T(1,128)} %param.49) | copy-start | bytes 768004
  7.3 1543.3 %copy-start.5 = (f32[1,1,250,256]{3,1,2,0:T(1,128)S(1)}, f32[1,1,250,256]{3,1,2,0:T(1,128)}, u32[]{:S(2)}) copy-start(f32[1,1,250,256]{3,1,2,0:T(1,128)} %param.50) | copy-start | bytes 768004
  7.3 610.4 %all-reduce.11.cloned.1.call-start = ((), (), s32[]{:S(2)}) async-start(), calls=%async_computation.2 | async-start | bytes 720896 | tf_op jit(solution)/shard_map/psum | solution.py:86
  189.5 1291.4 %all-reduce.9.cloned.1.call-start = ((), (), s32[]{:S(2)}) async-start(), calls=%async_computation.1 | async-start | bytes 720896 | tf_op jit(solution)/shard_map/psum | solution.py:86
  870.5 639.9 %all-gather.7.cloned.1.call-start = ((), (), s32[]{:S(2)}) async-start(), calls=%async_computation | async-start | bytes 8454144 | tf_op jit(solution)/shard_map/all_gather | solution.py:109
Sparse Core Ops, SparseCore 0:
  189.7 336.8 all-reduce.10
  870.6 329.9 all-reduce.8
  1203.8 142.4 all-gather.6
where the time goes:
time: 1580 us
  blocking collectives  1440 us (91%)
  matrix products  61.4 us (4%)
  other arithmetic  49 us (3%)
    psum x2, blocking collectives, on_device(): lax.psum((raw_rights[0], raw_rights[1], raw_rights[2]), ('rep', 'shard'))  834 us
    psum x2, blocking collectives, on_device(): lefts = [lax.psum(left_part, ('rep', 'tp')) for left_part in parts]  204 us
    psum x2, blocking collectives, on_device(): summed = lax.psum((grams[0], grams[1], grams[2]), 'shard')  187 us
    all_gather x1, blocking collectives, on_device(): lax.all_gather(flats_new[2], 'rep', axis=1, tiled=True)  88.8 us
    all_gather x1, blocking collectives, on_device(): lax.all_gather(emb_ids, ('rep', 'shard'), axis=1, tiled=True)  82 us
    dot_general x32, matrix products, one_block(): jnp.dot(one_hot, block_values, preferred_element_type=jnp.float32)  38.6 us
  transfers between devices with their start and end apart: 3, of which 0 were waited for; matrix products, arithmetic and copies ran while one was open for 2% of the time, Pallas kernels for 0%

commit v1 on v0

--- a/solution.py
+++ b/solution.py
@@ -105,7 +105,12 @@
     row_start = (shard_index * rep_count + rep_index) * block_rows
     initial = jnp.zeros((block_rows, row_width), jnp.float32)
     pieces = (
-        lax.all_gather(emb_ids, ("rep", "shard"), axis=1, tiled=True),
+        jnp.concatenate(
+            lax.all_to_all(
+                jnp.stack([emb_ids] * lax.axis_size(("rep", "shard"))), ("rep", "shard"), 0, 0
+            ),
+            axis=1,
+        ),
         lax.all_gather(emb_grad, ("rep", "shard"), axis=1, tiled=True),
     )
     row_ids = pieces[0].reshape(-1)

time: 1580 us -> 1510 us (0.956)
  blocking collectives: 1440 us -> 1360 us
  starting transfers between devices: 0.12 us -> 18.3 us
    all_gather x1 -> x0, blocking collectives: 82 us -> none  [on_device(): lax.all_gather(emb_ids, ('rep', 'shard'), axis=1, tiled=True)]
    all_to_all x0 -> x1, starting transfers between devices: none -> 18.2 us  [on_device(): lax.all_to_all(jnp.stack([emb_ids] * lax.axis_size(('rep', 'shard'))), ('...]
  transfers between devices with their start and end apart: 3 -> 4, of which waited for: 0 -> 0; matrix products, arithmetic and copies ran while one was open for 2% -> 2% of each run, Pallas kernels for 0% -> 0%
where the time goes in v1:
time: 1510 us
  blocking collectives  1360 us (90%)
  matrix products  61.4 us (4%)
  other arithmetic  49 us (3%)
  starting transfers between devices  18.3 us (1%)
    psum x2, blocking collectives, on_device(): lax.psum((raw_rights[0], raw_rights[1], raw_rights[2]), ('rep', 'shard'))  834 us
    psum x2, blocking collectives, on_device(): lefts = [lax.psum(left_part, ('rep', 'tp')) for left_part in parts]  204 us
    psum x2, blocking collectives, on_device(): summed = lax.psum((grams[0], grams[1], grams[2]), 'shard')  187 us
    all_gather x1, blocking collectives, on_device(): lax.all_gather(flats_new[2], 'rep', axis=1, tiled=True)  88.9 us
    dot_general x32, matrix products, one_block(): jnp.dot(one_hot, block_values, preferred_element_type=jnp.float32)  38.6 us
  transfers between devices with their start and end apart: 4, of which 0 were waited for; matrix products, arithmetic and copies ran while one was open for 2% of the time, Pallas kernels for 0%

profile of v1, /device:TPU:16, one launch (start us, length us, event | category | flops | bytes accessed | tf_op | source)
XLA Modules:
  0.0 1512.4 jit_solution(6474778436480141727)
XLA Ops:
  11.9 62.7 %all-reduce.5 = (f32[32,32]{1,0:T(8,128)S(1)}, f32[32,32]{1,0:T(8,128)S(1)}, f32[128,32]{0,1:T(8,128)S(1)}) all-reduce(f32[32,32]{1,0:T(8,128)S(1)} %fusion.29, f32[32,32]{1,0:T(8,128)S(1)} %fusion.11, f32[128,32]{0,1:T(8,128)S(1)} %fusion.20), channel_id=1, replica_groups=mesh['rep'=4,'shard'=32,'tp'=4] {'rep','tp'}, use_global_device_ids=true, to_apply=%region_0.0 | all-reduce | flops 6144 | bytes 49152 | tf_op jit(solution)/shard_map/psum | solution.py:78
  75.1 96.4 %all-reduce.3 = (f32[32,32]{0,1:T(8,128)S(1)}, f32[32,32]{0,1:T(8,128)S(1)}, f32[32,32]{0,1:T(8,128)S(1)}) all-reduce(f32[32,32]{0,1:T(8,128)S(1)} %fusion.68, f32[32,32]{0,1:T(8,128)S(1)} %fusion.70, f32[32,32]{0,1:T(8,128)S(1)} %fusion.72), channel_id=1, replica_groups=mesh['rep'=4,'shard'=32,'tp'=4] {'shard'}, use_global_device_ids=true, to_apply=%region_1.0 | all-reduce | flops 3072 | bytes 24576 | tf_op jit(solution)/shard_map/psum | solution.py:80
  171.7 2.9 cholesky.126
  176.0 2.4 custom-call.15
  178.7 2.1 fusion.9
  180.8 2.9 cholesky.104
  185.1 2.4 custom-call.13
  187.7 1.8 fusion.27
  189.6 2.9 cholesky.148
  193.8 2.4 custom-call.17
  197.6 418.9 %psum.147 = f32[256,32]{0,1:T(8,128)S(1)} all-reduce(f32[256,32]{0,1:T(8,128)S(1)} %fusion.18), channel_id=1, replica_groups=mesh['rep'=4,'shard'=32,'tp'=4] {'rep','shard'}, use_global_device_ids=true, to_apply=%region_16.0 | all-reduce | flops 8192 | bytes 65536 | tf_op jit(solution)/shard_map/psum | solution.py:86
  618.9 1.4 fusion.7
  620.3 141.7 %all-reduce.4 = (f32[32,32]{1,0:T(8,128)S(1)}, f32[32,32]{1,0:T(8,128)S(1)}, f32[128,32]{0,1:T(8,128)S(1)}) all-reduce(f32[32,32]{1,0:T(8,128)S(1)} %fusion.25, f32[32,32]{1,0:T(8,128)S(1)} %fusion.7, f32[128,32]{0,1:T(8,128)S(1)} %fusion.16), channel_id=1, replica_groups=mesh['rep'=4,'shard'=32,'tp'=4] {'rep','tp'}, use_global_device_ids=true, to_apply=%region_5.8 | all-reduce | flops 6144 | bytes 49152 | tf_op jit(solution)/shard_map/psum | solution.py:78
  762.6 90.1 %all-reduce.2 = (f32[32,32]{0,1:T(8,128)S(1)}, f32[32,32]{0,1:T(8,128)S(1)}, f32[32,32]{0,1:T(8,128)S(1)}) all-reduce(f32[32,32]{0,1:T(8,128)S(1)} %fusion.69, f32[32,32]{0,1:T(8,128)S(1)} %fusion.71, f32[32,32]{0,1:T(8,128)S(1)} %fusion.73), channel_id=1, replica_groups=mesh['rep'=4,'shard'=32,'tp'=4] {'shard'}, use_global_device_ids=true, to_apply=%region_6.9 | all-reduce | flops 3072 | bytes 24576 | tf_op jit(solution)/shard_map/psum | solution.py:80
  852.7 2.9 cholesky.137
  857.0 2.4 custom-call.16
  859.6 2.1 fusion.5
  861.8 2.9 cholesky.115
  866.0 2.4 custom-call.14
  868.7 1.8 fusion.23
  872.6 18.2 %all-to-all-start = ((s32[128,1,128]{2,1,0:T(1,128)}), s32[128,1,128]{2,1,0:T(1,128)S(1)}, u32[]{:S(2)}, u32[]{:S(2)}) async-start(s32[128,1,128]{2,1,0:T(1,128)} %stack.2), calls=%async_computation | async-start | bytes 131072 | tf_op jit(solution)/shard_map/all_to_all | solution.py:109
  891.4 8.5 psum.151
  901.2 2.9 cholesky.159
  905.5 2.4 custom-call.18
  909.2 415.4 %psum.150 = f32[256,32]{0,1:T(8,128)S(1)} all-reduce(f32[256,32]{0,1:T(8,128)S(1)} %fusion.14), channel_id=1, replica_groups=mesh['rep'=4,'shard'=32,'tp'=4] {'rep','shard'}, use_global_device_ids=true, to_apply=%region_19.23 | all-reduce | flops 8192 | bytes 65536 | tf_op jit(solution)/shard_map/psum | solution.py:86
  1325.0 1.4 fusion.66
  1326.4 88.9 %all-gather.2 = f32[128,256]{1,0:T(8,128)S(1)} all-gather(f32[32,256]{1,0:T(8,128)S(1)} %get-tuple-element.108), channel_id=4, replica_groups=mesh['rep'=4,'shard'=32,'tp'=4] {'rep'}, dimensions={0}, use_global_device_ids=true | all-gather | bytes 163840 | tf_op jit(solution)/shard_map/all_gather | solution.py:124
  1415.3 1.6 fusion.22
  1420.3 12.2 all-gather.1
  1434.4 11.9 all-gather
  1447.7 40.2 %while.11 = (s32[]{:T(128)}, f32[250,256]{1,0:T(8,128)S(1)}, s32[32,512]{1,0:T(8,128)S(1)}, s32[]{:T(128)}, bf16[32,512,256]{2,1,0:T(8,128)(2,1)}, /*index=5*/s32[]{:T(128)}, s32[]{:T(128)}) while((s32[]{:T(128)}, f32[250,256]{1,0:T(8,128)S(1)}, s32[32,512]{1,0:T(8,128)S(1)}, s32[]{:T(128)}, bf16[32,512,256]{2,1,0:T(8,128)(2,1)}, ...), condition=%wide.region_22.26_spmd.clone, body=%wide.region_21.25_spmd.clone.sunk | while | flops 65792512 | bytes 780895 | solution.py:37
  1488.0 13.8 all-gather.4
  (164 shorter events, 74.1 us)
Async XLA Ops:
  7.2 1.0 copy-start
  7.2 1439.8 %copy-start.2 = (bf16[1,32,2048]{2,1,0:T(8,128)(2,1)S(1)}, bf16[1,32,2048]{2,1,0:T(8,128)(2,1)}, u32[]{:S(2)}) copy-start(bf16[1,32,2048]{2,1,0:T(8,128)(2,1)} %param.34) | copy-start | bytes 393220
  7.2 1439.7 %copy-start.1 = (f32[1,32,2048]{2,1,0:T(8,128)S(1)}, f32[1,32,2048]{2,1,0:T(8,128)}, u32[]{:S(2)}) copy-start(f32[1,32,2048]{2,1,0:T(8,128)} %param.35) | copy-start | bytes 786436
  7.2 1439.1 %copy-start.4 = (bf16[1,32,768]{2,1,0:T(8,128)(2,1)S(1)}, bf16[1,32,768]{2,1,0:T(8,128)(2,1)}, u32[]{:S(2)}) copy-start(bf16[1,32,768]{2,1,0:T(8,128)(2,1)} %param.29) | copy-start | bytes 147460
  7.2 1439.1 %copy-start.3 = (f32[1,32,768]{2,1,0:T(8,128)S(1)}, f32[1,32,768]{2,1,0:T(8,128)}, u32[]{:S(2)}) copy-start(f32[1,32,768]{2,1,0:T(8,128)} %param.30) | copy-start | bytes 294916
  7.2 1412.4 %copy-start.8 = (f32[1,1,8,2048]{3,2,1,0:T(8,128)S(1)}, f32[1,1,8,2048]{3,2,1,0:T(8,128)}, u32[]{:S(2)}) copy-start(f32[1,1,8,2048]{3,2,1,0:T(8,128)} %param.37) | copy-start | bytes 196612
  7.3 1412.4 %copy-start.7 = (f32[1,1,8,2048]{3,2,1,0:T(8,128)S(1)}, f32[1,1,8,2048]{3,2,1,0:T(8,128)}, u32[]{:S(2)}) copy-start(f32[1,1,8,2048]{3,2,1,0:T(8,128)} %param.38) | copy-start | bytes 196612
  7.3 1426.5 %copy-start.10 = (f32[1,1,8,768]{3,2,1,0:T(8,128)S(1)}, f32[1,1,8,768]{3,2,1,0:T(8,128)}, u32[]{:S(2)}) copy-start(f32[1,1,8,768]{3,2,1,0:T(8,128)} %param.32) | copy-start | bytes 73732
  7.3 1426.5 %copy-start.9 = (f32[1,1,8,768]{3,2,1,0:T(8,128)S(1)}, f32[1,1,8,768]{3,2,1,0:T(8,128)}, u32[]{:S(2)}) copy-start(f32[1,1,8,768]{3,2,1,0:T(8,128)} %param.33) | copy-start | bytes 73732
  7.3 1480.6 %copy-start.6 = (f32[1,1,250,256]{3,1,2,0:T(1,128)S(1)}, f32[1,1,250,256]{3,1,2,0:T(1,128)}, u32[]{:S(2)}) copy-start(f32[1,1,250,256]{3,1,2,0:T(1,128)} %param.49) | copy-start | bytes 768004
  7.3 1480.6 %copy-start.5 = (f32[1,1,250,256]{3,1,2,0:T(1,128)S(1)}, f32[1,1,250,256]{3,1,2,0:T(1,128)}, u32[]{:S(2)}) copy-start(f32[1,1,250,256]{3,1,2,0:T(1,128)} %param.50) | copy-start | bytes 768004
  7.3 610.4 %all-reduce.11.cloned.1.call-start = ((), (), s32[]{:S(2)}) async-start(), calls=%async_computation.3 | async-start | bytes 720896 | tf_op jit(solution)/shard_map/psum | solution.py:86
  189.5 1228.7 %all-reduce.9.cloned.1.call-start = ((), (), s32[]{:S(2)}) async-start(), calls=%async_computation.2 | async-start | bytes 720896 | tf_op jit(solution)/shard_map/psum | solution.py:86
  870.5 577.2 %all-gather.7.cloned.1.call-start = ((), (), s32[]{:S(2)}) async-start(), calls=%async_computation.1 | async-start | bytes 8454144 | tf_op jit(solution)/shard_map/all_gather | solution.py:114
  872.6 544.3 %all-to-all-start = ((s32[128,1,128]{2,1,0:T(1,128)}), s32[128,1,128]{2,1,0:T(1,128)S(1)}, u32[]{:S(2)}, u32[]{:S(2)}) async-start(s32[128,1,128]{2,1,0:T(1,128)} %stack.2), calls=%async_computation | async-start | bytes 131072 | tf_op jit(solution)/shard_map/all_to_all | solution.py:109
Sparse Core Ops, SparseCore 0:
  189.7 336.8 all-reduce.10
  870.6 330.4 all-reduce.8
  1204.2 142.0 all-gather.6
